TPU v7x, 32 devices: a whole 2x2x4 slice. The times are simulated.
32 devices in a mesh: band: 2 (over x), feed: 16 (over z, y, core).
Axes of the slice: x: 2, y: 2, z: 4, core: 2. Of those that a mesh axis runs over, the one named last changes fastest.
Arguments:
- samples: int32 [8192, 16, 519], P(('band', 'feed')), parts along dimension 0, may hold values from 0 to 255
- gains: int32 [2, 32, 4096], P(None, 'band', 'feed'), parts along dimension 1, may hold values from -2048 to 2047
- feed_slot: int32 [4096], replicated, may hold values from 0 to 4095, each once
Outputs:
- visibility: float32 [8192, 2, 4096], P(('band', 'feed')), parts along dimension 0
There are 2 independent parts, one for each index of `band`. A program takes and returns all parts, laid end to end along the dimension named above; an argument that names none is the same for every part. Nothing has to cross between parts.
Inputs may be any that keep to these rules, and one draw needn't show every extreme that they name: `samples`: each word is 16 times the in-phase level plus the quadrature level, both offset by 8. `feed_slot`: every slot appears once.
All inputs are finite; a program needn't handle non-finite values.
Results may differ from a plain program's by a relative error of at most 0.0026.
Values may be sent and summed in bfloat16 or wider, within the bound.
A program may use at most 128 MiB of HBM per device.

v0:
```python
import math

import jax
import jax.numpy as jnp
from jax import lax
from jax.sharding import PartitionSpec as P

CH = 16
TAPS = 8
SPECTRA = 512
ROWS = 256


def filter_taps():
    length = TAPS * CH
    place = jnp.arange(length).astype(jnp.float32)
    window = 0.5 - 0.5 * jnp.cos(2.0 * math.pi * place / (length - 1))
    return (jnp.sinc((place - 0.5 * (length - 1)) / CH) * window).reshape(TAPS, CH)


def dft_table():
    index = jnp.arange(CH, dtype=jnp.int32)
    phase = index[:, None] * index[None, :] % CH
    angle = phase.astype(jnp.float32) * (2.0 * math.pi / CH)
    cosine = jnp.cos(angle) / math.sqrt(CH)
    sine = jnp.sin(angle) / math.sqrt(CH)
    upper = jnp.stack([cosine, sine], axis=1)
    lower = jnp.stack([-sine, cosine], axis=1)
    return jnp.stack([upper, lower], axis=0)


def channelize(words, scales, blocks):
    inphase = (words // 16 - 8).astype(jnp.float32) * 0.125
    quadrature = (words % 16 - 8).astype(jnp.float32) * 0.125
    voltage = jnp.stack([inphase, quadrature], axis=1)
    taps = filter_taps()
    count = words.shape[2] - TAPS + 1
    filtered = taps[0][None, None, :, None] * voltage[:, :, :, 0:count]
    for tap in range(1, TAPS):
        filtered = filtered + taps[tap][None, None, :, None] * voltage[:, :, :, tap : tap + count]
    split = filtered.reshape(filtered.shape[0], 2, CH, blocks, count // blocks)
    channels = jnp.einsum("pcqk,nqkat->canpt", dft_table(), split, precision=lax.Precision.HIGHEST)
    gain = scales.astype(jnp.float32) * (1.0 / 2048.0)
    gain_real = gain[0][:, None, :, None]
    gain_imag = gain[1][:, None, :, None]
    real = channels[:, :, :, 0]
    imag = channels[:, :, :, 1]
    weighted = jnp.stack(
        [gain_real * real - gain_imag * imag, gain_real * imag + gain_imag * real], axis=3
    )
    return weighted.astype(jnp.bfloat16)


def sky_order(moved, feed_slot):
    flat = moved.reshape(moved.shape[1], moved.shape[2] * moved.shape[3])
    return jnp.take(flat, feed_slot, axis=0)[None]


def correlate(stacked, first):
    feed_rows = lax.dynamic_slice_in_dim(stacked, first, ROWS, 1)
    middle = stacked.shape[2] // 2
    turned = jnp.concatenate([feed_rows[:, :, middle:], -feed_rows[:, :, :middle]], axis=2)
    left_side = jnp.stack([feed_rows, turned], axis=2)
    return jnp.einsum("mrok,mjk->roj", left_side, stacked, preferred_element_type=jnp.float32)


def body(samples, gains, feed_slot):
    groups = lax.axis_size("feed") // CH
    position = lax.axis_index("feed")
    first = position % groups * ROWS
    spectra = channelize(samples, gains, 1)
    copies = jnp.broadcast_to(spectra, (CH, groups) + spectra.shape[2:])
    outgoing = copies.reshape((CH * groups,) + spectra.shape[2:])
    moved = lax.all_to_all(outgoing, "feed", split_axis=0, concat_axis=1, tiled=True)
    total = correlate(sky_order(moved, feed_slot), first)
    return total * (1.0 / SPECTRA)


def solution(mesh):
    return jax.shard_map(
        body,
        mesh=mesh,
        in_specs=(P(("band", "feed"), None, None), P(None, "band", "feed"), P()),
        out_specs=P(("band", "feed"), None, None),
        check_vma=False,
    )
```

profile of v0, /device:TPU:13, one launch (start us, length us, event | category | flops | bytes accessed | tf_op | source)
XLA Modules:
  0.0 385.7 jit_solution(17009220216554379644)
XLA Ops:
  0.0 0.1 sine_multiply_fusion
  0.1 0.1 fusion.58
  0.2 0.1 fusion.68
  0.3 14.5 %fusion.30 = (f32[256,1,16,519]{0,2,3,1:T(8,128)}, f32[256,1,16,519]{0,2,3,1:T(8,128)}) fusion(s32[256,16,519]{0,1,2:T(8,128)} %param.3), kind=kLoop, calls=%fused_computation.52 | loop fusion | flops 53145600 | bytes 25509888 | tf_op jit(solution)/shard_map/stack | solution.py:35
  14.8 49.6 %fusion.4 = f32[256,2,16,512,1]{0,2,3,1,4:T(8,128)} fusion(f32[256,1,16,519]{0,2,3,1:T(8,128)} %get-tuple-element.6, f32[256,1,16,519]{0,2,3,1:T(8,128)} %get-tuple-element.5, f32[16]{0:T(128)S(1)} %get-tuple-element.16, f32[16]{0:T(128)S(1)} %get-tuple-element.17, f32[16]{0:T(128)S(1)} %get-tuple-element.18, f32[16]{0:T(128)S(1)} %get-tuple-element.19, ...), kind=kLoop, calls=%fused_computation.19 | loop fusion | flops 96468992 | bytes 33784320 | tf_op jit(solution)/shard_map/add | solution.py:40
  64.3 0.0 copy-start.1
  64.3 20.3 %copy.33 = f32[256,2,16,512,1]{3,2,1,4,0:T(8,128)} copy(f32[256,2,16,512,1]{0,2,3,1,4:T(8,128)} %fusion.4) | data formatting | bytes 33554432 | tf_op jit(solution)/shard_map/add | solution.py:40
  84.6 0.0 copy-done.1
  84.6 0.1 copy.22
  84.7 0.1 copy.25
  84.9 19.7 %convolution_bitcast_fusion = f32[16,1,256,2,512]{4,0,3,2,1:T(8,128)S(1)} fusion(f32[256,2,16,512,1]{3,2,1,4,0:T(8,128)} %copy.33, f32[1,16,2,16]{3,1,2,0:T(8,128)S(1)} %get-tuple-element.14, f32[1,16,2,16]{3,1,2,0:T(8,128)S(1)} %get-tuple-element.13), kind=kOutput, calls=%fused_computation.44 | convolution fusion | flops 1610613760 | bytes 33558528 | tf_op jit(solution)/shard_map/pcqk,nqkat->canpt/dot_general | solution.py:42
  104.5 1.8 fusion.42
  106.3 3.6 fusion.43
  109.9 6.3 %pad_maximum_fusion.1 = bf16[16,256,2,512]{3,0,1,2:T(8,128)(2,1)} fusion(bf16[16,256,1,512]{3,0,1,2:T(8,128)(2,1)} %fusion.43, bf16[16,256,1,512]{3,0,1,2:T(8,128)(2,1)S(1)} %fusion.42), kind=kLoop, calls=%fused_computation.56 | loop fusion | flops 4194304 | bytes 16777216 | tf_op jit(solution)/shard_map/stack | solution.py:48
  116.2 11.4 %copy.29 = bf16[16,256,2,512]{3,1,2,0:T(8,128)(2,1)} copy(bf16[16,256,2,512]{3,0,1,2:T(8,128)(2,1)} %pad_maximum_fusion.1) | data formatting | bytes 16777216 | tf_op jit(solution)/shard_map/stack | solution.py:48
  127.6 0.0 copy-start
  127.6 6.7 %all-to-all-start = ((bf16[16,256,2,512]{3,1,2,0:T(8,128)(2,1)}), bf16[16,256,2,512]{3,1,2,0:T(8,128)(2,1)}, u32[]{:S(2)}, u32[]{:S(2)}) async-start(bf16[16,256,2,512]{3,1,2,0:T(8,128)(2,1)} %copy.29), calls=%async_computation | async-start | bytes 16777216 | tf_op jit(solution)/shard_map/all_to_all | solution.py:74
  134.2 0.0 copy-done
  134.3 182.3 %all-to-all-done = bf16[16,256,2,512]{3,1,2,0:T(8,128)(2,1)} async-done(((bf16[16,256,2,512]{3,1,2,0:T(8,128)(2,1)}), bf16[16,256,2,512]{3,1,2,0:T(8,128)(2,1)}, u32[]{:S(2)}, u32[]{:S(2)}) %all-to-all-start) | async-done | bytes 8388640 | tf_op jit(solution)/shard_map/all_to_all | solution.py:74
  316.6 16.2 %copy.37 = bf16[16,256,2,512]{3,2,1,0:T(2,128)(2,1)} copy(bf16[16,256,2,512]{3,1,2,0:T(8,128)(2,1)} %all-to-all-done) | data formatting | bytes 16777216 | tf_op jit(solution)/shard_map/reshape | solution.py:55
  332.8 9.3 %copy.40 = bf16[512,8,2,512]{3,1,2,0:T(8,128)(2,1)} copy(bf16[512,8,2,512]{3,2,1,0:T(2,128)(2,1)} %bitcast.85) | data formatting | bytes 16777216
  342.1 25.2 %gather_fusion = bf16[4096,1024]{1,0:T(8,128)(2,1)} fusion(bf16[4096,1024]{1,0:T(8,128)(2,1)} %bitcast.84, s32[4096]{0:T(1024)S(1)} %fusion.51), kind=kCustom, calls=%fused_computation | custom fusion | bytes 16793600 | tf_op jit(solution)/shard_map/jit(_take)/gather | solution.py:56
  367.4 1.2 fusion.47
  368.6 0.1 maximum_bitcast_fusion.2
  368.7 7.2 %fusion.38 = f32[256,2,4096]{2,0,1:T(8,128)S(1)} fusion(bf16[4096,1024]{1,0:T(8,128)(2,1)} %gather_fusion, pred[4096]{0:T(1024)(128)(4,1)S(1)} %compare_and_fusion, bf16[1,256,1,1024]{3,1,2,0:T(8,128)(2,1)S(1)} %maximum_bitcast_fusion.2, bf16[1,256,1,1024]{3,1,2,0:T(8,128)(2,1)S(1)} %get-tuple-element.7), kind=kOutput, calls=%fused_computation.67 | convolution fusion | flops 4301783040 | bytes 17829888 | tf_op jit(solution)/shard_map/mrok,mjk->roj/dot_general | solution.py:64
  375.9 9.8 %copy.32 = f32[256,2,4096]{2,1,0:T(2,128)} copy(f32[256,2,4096]{2,0,1:T(8,128)S(1)} %fusion.38) | data formatting | bytes 16777216 | tf_op jit(solution)/shard_map/mul | solution.py:76
  (8 shorter events, 0.1 us)
Async XLA Ops:
  64.3 20.3 %copy-start.1 = (s32[2,16,256]{2,1,0:T(8,128)S(1)}, s32[2,16,256]{2,1,0:T(8,128)}, u32[]{:S(2)}) copy-start(s32[2,16,256]{2,1,0:T(8,128)} %param.4) | copy-start | bytes 98308
  127.6 6.7 %copy-start = (s32[4096]{0:T(1024)S(1)}, s32[4096]{0:T(1024)}, u32[]{:S(2)}) copy-start(s32[4096]{0:T(1024)} %param.5) | copy-start | bytes 49156
  127.6 189.0 %all-to-all-start = ((bf16[16,256,2,512]{3,1,2,0:T(8,128)(2,1)}), bf16[16,256,2,512]{3,1,2,0:T(8,128)(2,1)}, u32[]{:S(2)}, u32[]{:S(2)}) async-start(bf16[16,256,2,512]{3,1,2,0:T(8,128)(2,1)} %copy.29), calls=%async_computation | async-start | bytes 16777216 | tf_op jit(solution)/shard_map/all_to_all | solution.py:74
where the time goes:
time: 387 us; the launch traced here: 386 us
  waiting for transfers between devices  182 us (47%)
  local copies, waits for them, and re-layouts  92.5 us (24%)
  other arithmetic  77.2 us (20%)
  matrix products  26.9 us (7%)
  starting transfers between devices  6.65 us (2%)
    all_to_all x1, waiting for transfers between devices, body(): lax.all_to_all(outgoing, 'feed', split_axis=0, concat_axis=1, tiled=True)  182 us
    add x1, other arithmetic, channelize(): filtered + taps[tap][None, None, :, None] * voltage[:, :, :, tap:tap + co...  49.6 us
    gather x1, local copies, waits for them, and re-layouts, sky_order(): return jnp.take(flat, feed_slot, axis=0)[None]  25.2 us
    add x1, local copies, waits for them, and re-layouts, channelize(): filtered + taps[tap][None, None, :, None] * voltage[:, :, :, tap:tap + co...  20.3 us
    dot_general x1, matrix products, channelize(): jnp.einsum('pcqk,nqkat->canpt', dft_table(), split, precision=lax.Precisi...  19.7 us
    reshape x1, local copies, waits for them, and re-layouts, sky_order(): flat = moved.reshape(moved.shape[1], moved.shape[2] * moved.shape[3])  16.2 us
    another operation x1, other arithmetic, channelize(): voltage = jnp.stack([inphase, quadrature], axis=1)  14.5 us
    another operation x3, other arithmetic, channelize(): jnp.stack([gain_real * real - gain_imag * imag, gain_real * imag + gain_i...  11.7 us
  transfers between devices with their start and end apart: 1, of which 1 were waited for; matrix products, arithmetic and copies ran while one was open for 0% of the time, Pallas kernels for 0%

commit v1 on v0

v1 whole, which is shorter than its diff:
```python
import functools
import math

import jax
import jax.numpy as jnp
import numpy as np
from jax import lax
from jax.experimental import pallas as pl
from jax.experimental.pallas import tpu as pltpu
from jax.sharding import PartitionSpec as P

CH = 16
TAPS = 8
SPECTRA = 512
ROWS = 256
CHUNKS = 1
BLOCK = 16
TERMS = 3
LANES = 128


def filter_bank():
    length = TAPS * CH
    place = np.arange(length, dtype=np.float64)
    window = 0.5 - 0.5 * np.cos(2.0 * math.pi * place / (length - 1))
    taps = (np.sinc((place - 0.5 * (length - 1)) / CH) * window).reshape(TAPS, CH)
    index = np.arange(CH)
    angle = (index[:, None] * index[None, :] % CH) * (2.0 * math.pi / CH)
    cosine = np.cos(angle) / math.sqrt(CH)
    sine = np.sin(angle) / math.sqrt(CH)
    table = np.stack([np.stack([cosine, sine], 1), np.stack([-sine, cosine], 1)], 0)
    bank = table[:, :, None, :, :] * taps[None, None, :, None, :]
    bank = 0.125 * bank.reshape(2 * CH, TAPS * 2 * CH)
    terms = []
    for _ in range(TERMS):
        term = bank.astype(jnp.bfloat16)
        terms.append(term)
        bank = bank - term.astype(np.float64)
    return np.concatenate(terms, 0)


def channel_kernel(start, count, bank_ref, words_ref, gains_ref, out_ref, rows):
    bank = bank_ref[...]
    for n in range(BLOCK):
        words = words_ref[n]
        inphase = ((words >> 4) - 8).astype(jnp.float32).astype(jnp.bfloat16)
        quadrature = ((words & 15) - 8).astype(jnp.float32).astype(jnp.bfloat16)
        voltage = jnp.concatenate([inphase, quadrature], axis=0)
        shifted = [voltage[:, start + t : start + t + count] for t in range(TAPS)]
        stacked = jnp.concatenate(shifted, axis=0)
        parts = jnp.dot(bank, stacked, preferred_element_type=jnp.float32)
        total = parts[: 2 * CH]
        for term in range(1, TERMS):
            total = total + parts[2 * CH * term : 2 * CH * (term + 1)]
        for lane in range(count // LANES):
            piece = total[:, lane * LANES : (lane + 1) * LANES]
            rows[0, lane, n * CH : (n + 1) * CH, :] = piece[:CH]
            rows[1, lane, n * CH : (n + 1) * CH, :] = piece[CH:]
    gain = gains_ref[...].astype(jnp.float32) * (1.0 / 2048.0)
    for c in range(CH):
        gain_real = gain[0][:, c : c + 1]
        gain_imag = gain[1][:, c : c + 1]
        for lane in range(count // LANES):
            real = rows[0, lane, pl.ds(c, BLOCK, stride=CH), :]
            imag = rows[1, lane, pl.ds(c, BLOCK, stride=CH), :]
            place = lane * LANES
            upper = gain_real * real - gain_imag * imag
            lower = gain_real * imag + gain_imag * real
            out_ref[c, :, place : place + LANES] = upper.astype(jnp.bfloat16)
            out_ref[c, :, count + place : count + place + LANES] = lower.astype(jnp.bfloat16)


def channelize(words, gains, start, count):
    inputs, _, frames = words.shape
    bank = jnp.asarray(filter_bank())
    return pl.pallas_call(
        functools.partial(channel_kernel, start, count),
        out_shape=jax.ShapeDtypeStruct((CH, inputs, 2 * count), jnp.bfloat16),
        grid=(inputs // BLOCK,),
        in_specs=[
            pl.BlockSpec(bank.shape, lambda i: (0, 0)),
            pl.BlockSpec((BLOCK, CH, frames), lambda i: (i, 0, 0)),
            pl.BlockSpec((2, BLOCK, CH), lambda i: (0, i, 0)),
        ],
        out_specs=pl.BlockSpec((CH, BLOCK, 2 * count), lambda i: (0, i, 0)),
        scratch_shapes=[pltpu.VMEM((2, count // LANES, BLOCK * CH, LANES), jnp.float32)],
        cost_estimate=pl.CostEstimate(
            flops=2 * inputs * count * bank.shape[0] * bank.shape[1],
            bytes_accessed=4 * words.size + 4 * inputs * CH * count,
            transcendentals=0,
        ),
    )(bank, words, gains)


def body(samples, gains, feed_slot):
    groups = lax.axis_size("feed") // CH
    position = lax.axis_index("feed")
    first = position % groups * ROWS
    spectra = samples.shape[2] - TAPS + 1
    count = spectra // CHUNKS
    turned_gains = jnp.transpose(gains, (0, 2, 1))
    own = lax.dynamic_slice_in_dim(feed_slot, first, ROWS, 0)
    total = None
    for chunk in range(CHUNKS):
        weighted = channelize(samples, turned_gains, chunk * count, count)
        if groups > 1:
            copies = jnp.broadcast_to(weighted[:, None], (CH, groups) + weighted.shape[1:])
            weighted = copies.reshape((CH * groups,) + weighted.shape[1:])
        moved = lax.all_to_all(weighted, "feed", split_axis=0, concat_axis=0, tiled=True)
        flat = moved.reshape(moved.shape[0] * moved.shape[1], moved.shape[2])
        ordered = jnp.take(flat, feed_slot, axis=0, mode="clip")
        feed_rows = jnp.take(flat, own, axis=0, mode="clip") * (1.0 / spectra)
        real, imag = feed_rows[:, :count], feed_rows[:, count:]
        left = jnp.stack([feed_rows, jnp.concatenate([imag, -real], axis=1)], axis=1)
        product = jnp.einsum("rok,jk->roj", left, ordered, preferred_element_type=jnp.float32)
        total = product if total is None else total + product
    return total


def solution(mesh):
    return jax.shard_map(
        body,
        mesh=mesh,
        in_specs=(P(("band", "feed"), None, None), P(None, "band", "feed"), P()),
        out_specs=P(("band", "feed"), None, None),
        check_vma=False,
    )
```

time: 387 us -> 283 us (0.73)
  other arithmetic: 77.2 us -> 0.18 us
  local copies, waits for them, and re-layouts: 92.5 us -> 54.1 us
  Pallas kernels: 0 us -> 32 us
  matrix products: 26.9 us -> 6.97 us
    add x1 -> x0, other arithmetic: 49.6 us -> none  [channelize(): filtered + taps[tap][None, None, :, None] * voltage[:, :, :, tap:tap + co...]
    pallas_call x0 -> x1, Pallas kernels: none -> 32 us  [channelize(): pl.pallas_call(functools.partial(channel_kernel, start, count), out_shape...]
    another operation x7 -> x1, other arithmetic: 27.4 us -> 0.06 us  [body(): jnp.stack([feed_rows, jnp.concatenate([imag, -real], axis=1)], axis=1)]
    add x1 -> x0, local copies, waits for them, and re-layouts: 20.3 us -> none  [channelize(): filtered + taps[tap][None, None, :, None] * voltage[:, :, :, tap:tap + co...]
    dot_general x2 -> x1, matrix products: 26.9 us -> 6.97 us  [body(): jnp.einsum('rok,jk->roj', left, ordered, preferred_element_type=jnp.float32)]
    reshape x1 -> x0, local copies, waits for them, and re-layouts: 16.2 us -> none  [sky_order(): flat = moved.reshape(moved.shape[1], moved.shape[2] * moved.shape[3])]
    another operation x2 -> x0, local copies, waits for them, and re-layouts: 11.4 us -> none  [the longest x1 11.4 us: channelize(): jnp.stack([gain_real * real - gain_imag * imag, gain_real * imag + gain_i...]
    mul x4 -> x0, local copies, waits for them, and re-layouts: 10 us -> none  [the longest x1 9.82 us: body(): return total * (1.0 / SPECTRA)]
where the time goes in v1:
time: 283 us; the launch traced here: 282 us
  waiting for transfers between devices  182 us (64%)
  local copies, waits for them, and re-layouts  54.1 us (19%)
  Pallas kernels  32 us (11%)
  matrix products  6.97 us (2%)
  starting transfers between devices  6.65 us (2%)
    all_to_all x1, waiting for transfers between devices, body(): lax.all_to_all(weighted, 'feed', split_axis=0, concat_axis=0, tiled=True)  182 us
    pallas_call x1, Pallas kernels, channelize(): pl.pallas_call(functools.partial(channel_kernel, start, count), out_shape...  32 us
    gather x1, local copies, waits for them, and re-layouts, body(): ordered = jnp.take(flat, feed_slot, axis=0, mode='clip')  25.2 us
    unnamed x6, local copies, waits for them, and re-layouts  13 us
    dot_general x1, local copies, waits for them, and re-layouts, body(): jnp.einsum('rok,jk->roj', left, ordered, preferred_element_type=jnp.float32)  9.82 us
    dot_general x1, matrix products, body(): jnp.einsum('rok,jk->roj', left, ordered, preferred_element_type=jnp.float32)  6.97 us
    all_to_all x1, starting transfers between devices, body(): lax.all_to_all(weighted, 'feed', split_axis=0, concat_axis=0, tiled=True)  6.65 us
    gather x1, local copies, waits for them, and re-layouts, body(): feed_rows = jnp.take(flat, own, axis=0, mode='clip') * (1.0 / spectra)  6.02 us
  transfers between devices with their start and end apart: 1, of which 1 were waited for; matrix products, arithmetic and copies ran while one was open for 0% of the time, Pallas kernels for 0%

profile of v1, /device:TPU:13, one launch (start us, length us, event | category | flops | bytes accessed | tf_op | source)
XLA Modules:
  0.0 282.2 jit_solution(17949567041924799798)
XLA Ops:
  0.0 0.0 copy-start
  0.0 12.1 %copy.6.words_ref = s32[256,16,519]{2,1,0:T(8,128)} copy(s32[256,16,519]{0,1,2:T(8,128)} %param.4) | data formatting | bytes 17006592 | tf_op args[0]
  12.1 0.0 copy-done
  12.1 0.8 copy.5
  13.0 32.0 %shard_map.46 = bf16[16,256,1024]{2,1,0:T(8,128)(2,1)} custom-call(bf16[96,256]{1,0:T(8,128)(2,1)} %constant.22.clone.bank_ref, s32[256,16,519]{2,1,0:T(8,128)} %copy.6.words_ref, s32[2,256,16]{2,1,0:T(8,128)} %bitcast.9), custom_call_target="tpu_custom_call" | custom-call | flops 6442450944 | bytes 16891904 | tf_op jit(solution)/shard_map/pallas_call | solution.py:76
  45.0 0.0 slice-start
  45.0 0.0 copy-start.1
  45.0 6.7 %all-to-all-start = ((bf16[16,256,1024]{2,1,0:T(8,128)(2,1)}), bf16[16,256,1024]{2,1,0:T(8,128)(2,1)}, u32[]{:S(2)}, u32[]{:S(2)}) async-start(bf16[16,256,1024]{2,1,0:T(8,128)(2,1)} %shard_map.46), calls=%async_computation | async-start | bytes 16777216 | tf_op jit(solution)/shard_map/all_to_all | solution.py:109
  51.6 0.0 slice-done
  51.6 0.0 copy-done.1
  51.7 182.3 %all-to-all-done = bf16[16,256,1024]{2,1,0:T(8,128)(2,1)} async-done(((bf16[16,256,1024]{2,1,0:T(8,128)(2,1)}), bf16[16,256,1024]{2,1,0:T(8,128)(2,1)}, u32[]{:S(2)}, u32[]{:S(2)}) %all-to-all-start) | async-done | bytes 8388640 | tf_op jit(solution)/shard_map/all_to_all | solution.py:109
  234.0 6.0 %gather_fusion = bf16[256,1024]{1,0:T(8,128)(2,1)S(1)} fusion(bf16[4096,1024]{1,0:T(8,128)(2,1)} %bitcast.1, s32[1024]{0:T(1024)S(1)} %pad_clamp_fusion), kind=kCustom, calls=%fused_computation | custom fusion | bytes 1049600 | tf_op jit(solution)/shard_map/jit(_take)/gather | solution.py:112
  240.0 0.1 fusion.6
  240.1 25.2 %gather_fusion.1 = bf16[4096,1024]{1,0:T(8,128)(2,1)} fusion(bf16[4096,1024]{1,0:T(8,128)(2,1)} %bitcast.1, s32[4096]{0:T(1024)S(1)} %broadcast_clamp_fusion), kind=kCustom, calls=%fused_computation.1 | custom fusion | bytes 16793600 | tf_op jit(solution)/shard_map/jit(_take)/gather | solution.py:111
  265.3 0.1 maximum_bitcast_fusion
  265.4 7.0 %fusion = f32[256,2,4096]{2,0,1:T(8,128)S(1)} fusion(bf16[4096,1024]{1,0:T(8,128)(2,1)} %gather_fusion.1, bf16[256,1,1024]{2,0,1:T(8,128)(2,1)S(1)} %maximum_bitcast_fusion, bf16[256,1,1024]{2,0,1:T(8,128)(2,1)S(1)} %get-tuple-element.5), kind=kOutput, calls=%fused_computation.2 | convolution fusion | flops 4295491584 | bytes 17825792 | tf_op jit(solution)/shard_map/rok,jk->roj/dot_general | solution.py:115
  272.4 9.8 %copy.7 = f32[256,2,4096]{2,1,0:T(2,128)} copy(f32[256,2,4096]{2,0,1:T(8,128)S(1)} %fusion) | data formatting | bytes 16777216 | tf_op jit(solution)/shard_map/rok,jk->roj/dot_general | solution.py:115
  (3 shorter events, 0.0 us)
Async XLA Ops:
  0.0 12.1 %copy-start = (s32[2,16,256]{2,1,0:T(8,128)S(1)}, s32[2,16,256]{2,1,0:T(8,128)}, u32[]{:S(2)}) copy-start(s32[2,16,256]{2,1,0:T(8,128)} %param.5) | copy-start | bytes 98308
  45.0 6.7 %slice-start = ((s32[4096]{0:T(1024)}), s32[256]{0:T(256)S(1)}, s32[]{:S(2)}) async-start(s32[4096]{0:T(1024)} %param.6), calls=%async_computation.1 | async-start | bytes 2048 | tf_op jit(solution)/shard_map/dynamic_slice | solution.py:102
  45.0 6.7 %copy-start.1 = (s32[4096]{0:T(1024)S(1)}, s32[4096]{0:T(1024)}, u32[]{:S(2)}) copy-start(s32[4096]{0:T(1024)} %param.6) | copy-start | bytes 49156
  45.0 189.0 %all-to-all-start = ((bf16[16,256,1024]{2,1,0:T(8,128)(2,1)}), bf16[16,256,1024]{2,1,0:T(8,128)(2,1)}, u32[]{:S(2)}, u32[]{:S(2)}) async-start(bf16[16,256,1024]{2,1,0:T(8,128)(2,1)} %shard_map.46), calls=%async_computation | async-start | bytes 16777216 | tf_op jit(solution)/shard_map/all_to_all | solution.py:109

commit v2 on v1

v2 whole, which is shorter than its diff:
```python
import functools
import math

import jax
import jax.numpy as jnp
import numpy as np
from jax import lax
from jax.experimental import pallas as pl
from jax.experimental.pallas import tpu as pltpu
from jax.sharding import PartitionSpec as P

CH = 16
TAPS = 8
SPECTRA = 512
ROWS = 256
CHUNKS = 4
SPAN = 32
TILE = 512
TERMS = 3
LANES = 128


def filter_bank():
    length = TAPS * CH
    place = np.arange(length, dtype=np.float64)
    window = 0.5 - 0.5 * np.cos(2.0 * math.pi * place / (length - 1))
    taps = (np.sinc((place - 0.5 * (length - 1)) / CH) * window).reshape(TAPS, CH)
    index = np.arange(CH)
    angle = (index[:, None] * index[None, :] % CH) * (2.0 * math.pi / CH)
    cosine = np.cos(angle) / math.sqrt(CH)
    sine = np.sin(angle) / math.sqrt(CH)
    table = np.stack([np.stack([cosine, sine], 1), np.stack([-sine, cosine], 1)], 0)
    bank = table[:, :, None, :, :] * taps[None, None, :, None, :]
    bank = 0.125 * bank.reshape(2 * CH, TAPS * 2 * CH)
    terms = []
    for _ in range(TERMS):
        term = bank.astype(jnp.bfloat16)
        terms.append(term)
        bank = bank - term.astype(np.float64)
    return np.concatenate(terms, 0)


def channel_kernel(bank_ref, words_ref, tail_ref, gains_ref, out_ref, voltage, rows):
    bank = bank_ref[...]
    span = out_ref.shape[2]

    def unpack(words):
        inphase = ((words >> 4) - 8).astype(jnp.float32).astype(jnp.bfloat16)
        quadrature = ((words & 15) - 8).astype(jnp.float32).astype(jnp.bfloat16)
        return jnp.concatenate([inphase, quadrature], axis=0)

    for m in range(span):
        voltage[m * 2 * CH : (m + 1) * 2 * CH, :] = unpack(words_ref[m])
    for m in range(TAPS - 1):
        place = (span + m) * 2 * CH
        voltage[place : place + 2 * CH, :] = unpack(tail_ref[m])
    gain = gains_ref[...].astype(jnp.float32) * (1.0 / 2048.0)
    for s in range(span):
        window = voltage[s * 2 * CH : (s + TAPS) * 2 * CH, :]
        parts = jnp.dot(bank, window, preferred_element_type=jnp.float32)
        total = parts[: 2 * CH]
        for term in range(1, TERMS):
            total = total + parts[2 * CH * term : 2 * CH * (term + 1)]
        real, imag = total[:CH], total[CH:]
        upper = gain[0] * real - gain[1] * imag
        lower = gain[0] * imag + gain[1] * real
        for lane in range(upper.shape[1] // LANES):
            place = slice(lane * LANES, (lane + 1) * LANES)
            rows[0, lane, s * CH : (s + 1) * CH, :] = upper[:, place]
            rows[1, lane, s * CH : (s + 1) * CH, :] = lower[:, place]
    for c in range(CH):
        for part in range(2):
            for lane in range(out_ref.shape[3] // LANES):
                place = slice(lane * LANES, (lane + 1) * LANES)
                piece = rows[part, lane, pl.ds(c, span, stride=CH), :]
                out_ref[c, part, :, place] = piece.astype(jnp.bfloat16)


def channelize(words, gains, start, count):
    inputs = words.shape[2]
    bank = jnp.asarray(filter_bank())
    span = min(SPAN, count)
    skip = start // span
    return pl.pallas_call(
        channel_kernel,
        out_shape=jax.ShapeDtypeStruct((CH, 2, count, inputs), jnp.bfloat16),
        grid=(count // span,),
        in_specs=[
            pl.BlockSpec(bank.shape, lambda i: (0, 0)),
            pl.BlockSpec((span, CH, inputs), lambda i: (skip + i, 0, 0)),
            pl.BlockSpec((8, CH, inputs), lambda i: ((skip + i + 1) * (span // 8), 0, 0)),
            pl.BlockSpec(gains.shape, lambda i: (0, 0, 0)),
        ],
        out_specs=pl.BlockSpec((CH, 2, span, inputs), lambda i: (0, 0, i, 0)),
        scratch_shapes=[
            pltpu.VMEM(((span + TAPS) * 2 * CH, inputs), jnp.bfloat16),
            pltpu.VMEM((2, inputs // LANES, span * CH, LANES), jnp.float32),
        ],
        cost_estimate=pl.CostEstimate(
            flops=2 * inputs * count * bank.shape[0] * bank.shape[1],
            bytes_accessed=4 * words.shape[1] * inputs * count + 4 * inputs * CH * count,
            transcendentals=0,
        ),
    )(bank, words, words, gains)


def product_kernel(scale, has_total, moved_ref, slot_ref, own_ref, *refs):
    out_ref, left = refs[-2], refs[-1]
    sources, depth, width = moved_ref.shape

    def pick(columns):
        total = None
        for source in range(sources):
            place = lax.broadcasted_iota(jnp.int32, (width, columns.shape[1]), 0) + source * width
            hot = jnp.where(place == columns, 1.0, 0.0).astype(jnp.bfloat16)
            part = jnp.dot(moved_ref[source], hot, preferred_element_type=jnp.float32)
            total = part if total is None else total + part
        return total

    @pl.when(pl.program_id(0) == 0)
    def _():
        feed_rows = jnp.transpose(pick(own_ref[...])) * scale
        real, imag = feed_rows[:, : depth // 2], feed_rows[:, depth // 2 :]
        left[0] = jnp.concatenate([real, imag], axis=1).astype(jnp.bfloat16)
        left[1] = jnp.concatenate([imag, -real], axis=1).astype(jnp.bfloat16)

    ordered = pick(slot_ref[...]).astype(jnp.bfloat16)
    for part in range(2):
        product = jnp.dot(left[part], ordered, preferred_element_type=jnp.float32)
        if has_total:
            product = product + refs[0][:, part, :]
        out_ref[:, part, :] = product


def correlate(moved, feed_slot, own, total, scale):
    sources, depth, width = moved.shape
    feeds = sources * width
    tile = min(TILE, feeds)
    block = pl.BlockSpec((ROWS, 2, tile), lambda j: (0, 0, j))
    return pl.pallas_call(
        functools.partial(product_kernel, scale, total is not None),
        out_shape=jax.ShapeDtypeStruct((ROWS, 2, feeds), jnp.float32),
        grid=(feeds // tile,),
        in_specs=[
            pl.BlockSpec(moved.shape, lambda j: (0, 0, 0)),
            pl.BlockSpec((1, tile), lambda j: (0, j)),
            pl.BlockSpec((1, ROWS), lambda j: (0, 0)),
        ]
        + ([] if total is None else [block]),
        out_specs=block,
        scratch_shapes=[pltpu.VMEM((2, ROWS, depth), jnp.bfloat16)],
        input_output_aliases={} if total is None else {3: 0},
        cost_estimate=pl.CostEstimate(
            flops=2 * depth * feeds * (feeds + 2 * ROWS),
            bytes_accessed=2 * moved.size + 8 * ROWS * feeds,
            transcendentals=0,
        ),
    )(moved, feed_slot[None], own[None], *([] if total is None else [total]))


def body(samples, gains, feed_slot):
    groups = lax.axis_size("feed") // CH
    position = lax.axis_index("feed")
    first = position % groups * ROWS
    inputs = samples.shape[0]
    spectra = samples.shape[2] - TAPS + 1
    count = spectra // CHUNKS
    words = jnp.transpose(samples, (2, 1, 0))
    spare = -inputs % LANES
    if spare:
        words = jnp.pad(words, ((0, 0), (0, 0), (0, spare)))
        gains = jnp.pad(gains, ((0, 0), (0, 0), (0, spare)))
    own = lax.dynamic_slice_in_dim(feed_slot, first, ROWS, 0)
    total = None
    for chunk in range(CHUNKS):
        weighted = channelize(words, gains, chunk * count, count)
        weighted = weighted.reshape(CH, 2 * count, inputs + spare)[:, :, :inputs]
        if groups > 1:
            copies = jnp.broadcast_to(weighted[:, None], (CH, groups) + weighted.shape[1:])
            weighted = copies.reshape((CH * groups,) + weighted.shape[1:])
        moved = lax.all_to_all(weighted, "feed", split_axis=0, concat_axis=0, tiled=True)
        total = correlate(moved, feed_slot, own, total, 1.0 / spectra)
    return total


def solution(mesh):
    return jax.shard_map(
        body,
        mesh=mesh,
        in_specs=(P(("band", "feed"), None, None), P(None, "band", "feed"), P()),
        out_specs=P(("band", "feed"), None, None),
        check_vma=False,
    )
```

time: 283 us -> 245 us (0.87)
  Pallas kernels: 32 us -> 95.7 us
  waiting for transfers between devices: 182 us -> 123 us
  local copies, waits for them, and re-layouts: 54.1 us -> 3.89 us
  starting transfers between devices: 6.65 us -> 20.8 us
  matrix products: 6.97 us -> 0 us
    pallas_call x1 -> x8, Pallas kernels: 32 us -> 95.7 us  [the longest x4 70.2 us: correlate(): pl.pallas_call(functools.partial(product_kernel, scale, total is not None...]
    all_to_all x1 -> x4, waiting for transfers between devices: 182 us -> 123 us  [body(): lax.all_to_all(weighted, 'feed', split_axis=0, concat_axis=0, tiled=True)]
    gather x2 -> x0, local copies, waits for them, and re-layouts: 31.3 us -> none  [the longest x1 25.2 us: body(): ordered = jnp.take(flat, feed_slot, axis=0, mode='clip')]
    all_to_all x1 -> x4, starting transfers between devices: 6.65 us -> 20.8 us  [body(): lax.all_to_all(weighted, 'feed', split_axis=0, concat_axis=0, tiled=True)]
    unnamed x6 -> x4, local copies, waits for them, and re-layouts: 13 us -> 2.68 us
    dot_general x1 -> x0, local copies, waits for them, and re-layouts: 9.82 us -> none  [body(): jnp.einsum('rok,jk->roj', left, ordered, preferred_element_type=jnp.float32)]
    dot_general x1 -> x0, matrix products: 6.97 us -> none  [body(): jnp.einsum('rok,jk->roj', left, ordered, preferred_element_type=jnp.float32)]
  transfers between devices with their start and end apart: 1 -> 4, of which waited for: 1 -> 3; matrix products, arithmetic and copies ran while one was open for 0% -> 0% of each run, Pallas kernels for 0% -> 29%
where the time goes in v2:
time: 245 us; the launch traced here: 244 us
  waiting for transfers between devices  123 us (50%)
  Pallas kernels  95.7 us (39%)
  starting transfers between devices  20.8 us (8%)
  local copies, waits for them, and re-layouts  3.89 us (2%)
    all_to_all x4, waiting for transfers between devices, body(): lax.all_to_all(weighted, 'feed', split_axis=0, concat_axis=0, tiled=True)  123 us
    pallas_call x4, Pallas kernels, correlate(): pl.pallas_call(functools.partial(product_kernel, scale, total is not None...  70.2 us
    pallas_call x4, Pallas kernels, channelize(): pl.pallas_call(channel_kernel, out_shape=jax.ShapeDtypeStruct((CH, 2, cou...  25.5 us
    all_to_all x4, starting transfers between devices, body(): lax.all_to_all(weighted, 'feed', split_axis=0, concat_axis=0, tiled=True)  20.8 us
  transfers between devices with their start and end apart: 4, of which 3 were waited for; matrix products, arithmetic and copies ran while one was open for 0% of the time, Pallas kernels for 29%

profile of v2, /device:TPU:13, one launch (start us, length us, event | category | flops | bytes accessed | tf_op | source)
XLA Modules:
  0.0 243.6 jit_solution(8622749771231040963)
XLA Ops:
  0.0 6.3 %shard_map.76 = bf16[16,2,128,256]{3,2,1,0:T(8,128)(2,1)} custom-call(bf16[96,256]{1,0:T(8,128)(2,1)} %constant.20.clone.bank_ref, s32[519,16,256]{2,1,0:T(8,128)} %bitcast.7, s32[519,16,256]{2,1,0:T(8,128)} %bitcast.8, s32[2,16,256]{2,1,0:T(8,128)} %gains_ref.7), custom_call_target="tpu_custom_call" | custom-call | flops 1610612736 | bytes 4194304 | tf_op jit(solution)/shard_map/pallas_call | solution.py:84
  6.3 6.5 %all-to-all-start.3 = ((bf16[16,256,256]{2,1,0:T(8,128)(2,1)}), bf16[16,256,256]{2,1,0:T(8,128)(2,1)S(1)}, u32[]{:S(2)}, u32[]{:S(2)}) async-start(bf16[16,256,256]{2,1,0:T(8,128)(2,1)} %bitcast.18), calls=%async_computation.3 | async-start | bytes 4194304 | tf_op jit(solution)/shard_map/all_to_all | solution.py:181
  12.8 6.4 %shard_map.75 = bf16[16,2,128,256]{3,2,1,0:T(8,128)(2,1)} custom-call(bf16[96,256]{1,0:T(8,128)(2,1)} %constant.20.clone.bank_ref, s32[519,16,256]{2,1,0:T(8,128)} %bitcast.9, s32[519,16,256]{2,1,0:T(8,128)} %bitcast.10, s32[2,16,256]{2,1,0:T(8,128)} %gains_ref.7), custom_call_target="tpu_custom_call" | custom-call | flops 1610612736 | bytes 4194304 | tf_op jit(solution)/shard_map/pallas_call | solution.py:84
  19.2 41.0 %all-to-all-done.3.moved_ref = bf16[16,256,256]{2,1,0:T(8,128)(2,1)S(1)} async-done(((bf16[16,256,256]{2,1,0:T(8,128)(2,1)}), bf16[16,256,256]{2,1,0:T(8,128)(2,1)S(1)}, u32[]{:S(2)}, u32[]{:S(2)}) %all-to-all-start.3) | async-done | bytes 2097184 | tf_op jit(solution)/shard_map/all_to_all | solution.py:181
  60.2 0.0 copy-start
  60.2 1.3 copy-done
  61.5 4.8 %all-to-all-start.2 = ((bf16[16,256,256]{2,1,0:T(8,128)(2,1)}), bf16[16,256,256]{2,1,0:T(8,128)(2,1)}, u32[]{:S(2)}, u32[]{:S(2)}) async-start(bf16[16,256,256]{2,1,0:T(8,128)(2,1)} %bitcast.17), calls=%async_computation.2 | async-start | bytes 4194304 | tf_op jit(solution)/shard_map/all_to_all | solution.py:181
  66.3 6.3 %shard_map.74 = bf16[16,2,128,256]{3,2,1,0:T(8,128)(2,1)} custom-call(bf16[96,256]{1,0:T(8,128)(2,1)} %constant.20.clone.bank_ref, s32[519,16,256]{2,1,0:T(8,128)} %bitcast.11, s32[519,16,256]{2,1,0:T(8,128)} %bitcast.12, s32[2,16,256]{2,1,0:T(8,128)} %gains_ref.7), custom_call_target="tpu_custom_call" | custom-call | flops 1610612736 | bytes 4194304 | tf_op jit(solution)/shard_map/pallas_call | solution.py:84
  72.7 41.2 %all-to-all-done.2.moved_ref = bf16[16,256,256]{2,1,0:T(8,128)(2,1)} async-done(((bf16[16,256,256]{2,1,0:T(8,128)(2,1)}), bf16[16,256,256]{2,1,0:T(8,128)(2,1)}, u32[]{:S(2)}, u32[]{:S(2)}) %all-to-all-start.2) | async-done | bytes 2097184 | tf_op jit(solution)/shard_map/all_to_all | solution.py:181
  113.9 4.8 %all-to-all-start.1 = ((bf16[16,256,256]{2,1,0:T(8,128)(2,1)}), bf16[16,256,256]{2,1,0:T(8,128)(2,1)S(1)}, u32[]{:S(2)}, u32[]{:S(2)}) async-start(bf16[16,256,256]{2,1,0:T(8,128)(2,1)} %bitcast.16), calls=%async_computation.1 | async-start | bytes 4194304 | tf_op jit(solution)/shard_map/all_to_all | solution.py:181
  118.6 6.4 %shard_map.73 = bf16[16,2,128,256]{3,2,1,0:T(8,128)(2,1)} custom-call(bf16[96,256]{1,0:T(8,128)(2,1)} %constant.20.clone.bank_ref, s32[519,16,256]{2,1,0:T(8,128)} %bitcast.13, s32[519,16,256]{2,1,0:T(8,128)} %bitcast.14, s32[2,16,256]{2,1,0:T(8,128)} %gains_ref.7), custom_call_target="tpu_custom_call" | custom-call | flops 1610612736 | bytes 4194304 | tf_op jit(solution)/shard_map/pallas_call | solution.py:84
  125.0 41.0 %all-to-all-done.1.moved_ref = bf16[16,256,256]{2,1,0:T(8,128)(2,1)S(1)} async-done(((bf16[16,256,256]{2,1,0:T(8,128)(2,1)}), bf16[16,256,256]{2,1,0:T(8,128)(2,1)S(1)}, u32[]{:S(2)}, u32[]{:S(2)}) %all-to-all-start.1) | async-done | bytes 2097184 | tf_op jit(solution)/shard_map/all_to_all | solution.py:181
  166.0 0.0 copy-start.1
  166.1 1.4 copy-done.1
  167.4 4.8 %all-to-all-start = ((bf16[16,256,256]{2,1,0:T(8,128)(2,1)}), bf16[16,256,256]{2,1,0:T(8,128)(2,1)}, u32[]{:S(2)}, u32[]{:S(2)}) async-start(bf16[16,256,256]{2,1,0:T(8,128)(2,1)} %bitcast.15), calls=%async_computation | async-start | bytes 4194304 | tf_op jit(solution)/shard_map/all_to_all | solution.py:181
  172.2 1.2 dynamic_slice.3
  173.4 16.2 %shard_map.77.refs_0_ = f32[256,2,4096]{2,1,0:T(2,128)} custom-call(bf16[16,256,256]{2,1,0:T(8,128)(2,1)} %copy-done, s32[1,4096]{1,0:T(1,128)} %bitcast.23, s32[1,256]{1,0:T(1,128)} %bitcast.19), custom_call_target="tpu_custom_call" | custom-call | flops 9663676416 | bytes 10485760 | tf_op jit(solution)/shard_map/pallas_call | solution.py:140
  189.6 18.0 %shard_map.78.refs_0_ = f32[256,2,4096]{2,1,0:T(2,128)} custom-call(bf16[16,256,256]{2,1,0:T(8,128)(2,1)} %all-to-all-done.2.moved_ref, s32[1,4096]{1,0:T(1,128)} %bitcast.24, s32[1,256]{1,0:T(1,128)} %bitcast.20, f32[256,2,4096]{2,1,0:T(2,128)} %shard_map.77.refs_0_), custom_call_target="tpu_custom_call", output_to_operand_aliasing={{}: (3, {})} | custom-call | flops 9663676416 | bytes 10485760 | tf_op jit(solution)/shard_map/pallas_call | solution.py:140
  207.6 18.0 %shard_map.79.refs_0_ = f32[256,2,4096]{2,1,0:T(2,128)} custom-call(bf16[16,256,256]{2,1,0:T(8,128)(2,1)} %copy-done.1, s32[1,4096]{1,0:T(1,128)} %bitcast.25, s32[1,256]{1,0:T(1,128)} %bitcast.21, f32[256,2,4096]{2,1,0:T(2,128)} %shard_map.78.refs_0_), custom_call_target="tpu_custom_call", output_to_operand_aliasing={{}: (3, {})} | custom-call | flops 9663676416 | bytes 10485760 | tf_op jit(solution)/shard_map/pallas_call | solution.py:140
  225.6 0.0 all-to-all-done.moved_ref
  225.6 18.0 %shard_map.80 = f32[256,2,4096]{2,1,0:T(2,128)} custom-call(bf16[16,256,256]{2,1,0:T(8,128)(2,1)} %all-to-all-done.moved_ref, s32[1,4096]{1,0:T(1,128)} %bitcast.26, s32[1,256]{1,0:T(1,128)} %bitcast.22, f32[256,2,4096]{2,1,0:T(2,128)} %shard_map.79.refs_0_), custom_call_target="tpu_custom_call", output_to_operand_aliasing={{}: (3, {})} | custom-call | flops 9663676416 | bytes 10485760 | tf_op jit(solution)/shard_map/pallas_call | solution.py:140
Async XLA Ops:
  6.3 53.9 %all-to-all-start.3 = ((bf16[16,256,256]{2,1,0:T(8,128)(2,1)}), bf16[16,256,256]{2,1,0:T(8,128)(2,1)S(1)}, u32[]{:S(2)}, u32[]{:S(2)}) async-start(bf16[16,256,256]{2,1,0:T(8,128)(2,1)} %bitcast.18), calls=%async_computation.3 | async-start | bytes 4194304 | tf_op jit(solution)/shard_map/all_to_all | solution.py:181
  60.2 1.3 copy-start
  61.5 52.3 %all-to-all-start.2 = ((bf16[16,256,256]{2,1,0:T(8,128)(2,1)}), bf16[16,256,256]{2,1,0:T(8,128)(2,1)}, u32[]{:S(2)}, u32[]{:S(2)}) async-start(bf16[16,256,256]{2,1,0:T(8,128)(2,1)} %bitcast.17), calls=%async_computation.2 | async-start | bytes 4194304 | tf_op jit(solution)/shard_map/all_to_all | solution.py:181
  113.9 52.2 %all-to-all-start.1 = ((bf16[16,256,256]{2,1,0:T(8,128)(2,1)}), bf16[16,256,256]{2,1,0:T(8,128)(2,1)S(1)}, u32[]{:S(2)}, u32[]{:S(2)}) async-start(bf16[16,256,256]{2,1,0:T(8,128)(2,1)} %bitcast.16), calls=%async_computation.1 | async-start | bytes 4194304 | tf_op jit(solution)/shard_map/all_to_all | solution.py:181
  166.0 1.4 copy-start.1
  167.4 58.2 %all-to-all-start = ((bf16[16,256,256]{2,1,0:T(8,128)(2,1)}), bf16[16,256,256]{2,1,0:T(8,128)(2,1)}, u32[]{:S(2)}, u32[]{:S(2)}) async-start(bf16[16,256,256]{2,1,0:T(8,128)(2,1)} %bitcast.15), calls=%async_computation | async-start | bytes 4194304 | tf_op jit(solution)/shard_map/all_to_all | solution.py:181

commit v3 on v1

v3 whole, which is shorter than its diff:
```python
import functools
import math

import jax
import jax.numpy as jnp
import numpy as np
from jax import lax
from jax.experimental import pallas as pl
from jax.experimental.pallas import tpu as pltpu
from jax.sharding import PartitionSpec as P

CH = 16
TAPS = 8
SPECTRA = 512
ROWS = 256
SHARES = (4, 5, 5, 2)
SPAN = 32
TILE = 512
TERMS = 3
LANES = 128


def filter_bank():
    length = TAPS * CH
    place = np.arange(length, dtype=np.float64)
    window = 0.5 - 0.5 * np.cos(2.0 * math.pi * place / (length - 1))
    taps = (np.sinc((place - 0.5 * (length - 1)) / CH) * window).reshape(TAPS, CH)
    index = np.arange(CH)
    angle = (index[:, None] * index[None, :] % CH) * (2.0 * math.pi / CH)
    cosine = np.cos(angle) / math.sqrt(CH)
    sine = np.sin(angle) / math.sqrt(CH)
    table = np.stack([np.stack([cosine, sine], 1), np.stack([-sine, cosine], 1)], 0)
    bank = table[:, :, None, :, :] * taps[None, None, :, None, :]
    bank = 0.125 * bank.reshape(2 * CH, TAPS * 2 * CH)
    terms = []
    for _ in range(TERMS):
        term = bank.astype(jnp.bfloat16)
        terms.append(term)
        bank = bank - term.astype(np.float64)
    return np.concatenate(terms, 0)


def unpack(words):
    inphase = ((words >> 4) - 8).astype(jnp.float32).astype(jnp.bfloat16)
    quadrature = ((words & 15) - 8).astype(jnp.float32).astype(jnp.bfloat16)
    return jnp.concatenate([inphase, quadrature], axis=0)


def pick(moved_ref, columns):
    sources, _, width = moved_ref.shape
    total = None
    for source in range(sources):
        place = lax.broadcasted_iota(jnp.int32, (width, columns.shape[1]), 0) + source * width
        hot = jnp.where(place == columns, 1.0, 0.0).astype(jnp.bfloat16)
        part = jnp.dot(moved_ref[source], hot, preferred_element_type=jnp.float32)
        total = part if total is None else total + part
    return total


def set_left(left, moved_ref, columns, scale):
    depth = moved_ref.shape[1]
    feed_rows = jnp.transpose(pick(moved_ref, columns)) * scale
    real, imag = feed_rows[:, : depth // 2], feed_rows[:, depth // 2 :]
    left[0, :, :depth] = jnp.concatenate([real, imag], axis=1).astype(jnp.bfloat16)
    left[1, :, :depth] = jnp.concatenate([imag, -real], axis=1).astype(jnp.bfloat16)


def exchange_kernel(counts, groups, scale, bank_ref, words_hbm, gains_ref, slot_ref, own_ref, *refs):
    chunks = len(counts)
    last_hbm, total_hbm = refs[:2]
    words_bufs = refs[2 : 2 + chunks]
    send_bufs = refs[2 + chunks : 2 + 2 * chunks]
    hold_bufs = refs[2 + 2 * chunks : 1 + 3 * chunks]
    voltage, rows, total, left, word_sem, own_sem, total_sem, send_sem, recv_sem = refs[1 + 3 * chunks :]
    targets = hold_bufs + (last_hbm,)
    me = lax.axis_index("feed")
    size = lax.axis_size("feed")
    inputs = send_bufs[0].shape[2]
    bank = bank_ref[...]
    gain = gains_ref[...].astype(jnp.float32) * (1.0 / 2048.0)

    barrier = pltpu.get_barrier_semaphore()

    def greet(d, carry):
        pl.semaphore_signal(
            barrier, inc=1, device_id={"feed": (me + d) % size}, device_id_type=pl.DeviceIdType.MESH
        )
        return carry

    lax.fori_loop(1, size, greet, 0)

    def word_copy(k):
        source = words_hbm.at[pl.ds(sum(counts[:k]), counts[k] + TAPS - 1)]
        return pltpu.make_async_copy(source, words_bufs[k], word_sem.at[k])

    def own_copy(k):
        return pltpu.make_async_copy(send_bufs[k].at[me // groups], targets[k].at[me], own_sem.at[k])

    def remote(k, d):
        there = (me + d) % size
        return pltpu.make_async_remote_copy(
            src_ref=send_bufs[k].at[there // groups],
            dst_ref=targets[k].at[me],
            send_sem=send_sem.at[k, d],
            recv_sem=recv_sem.at[k, d],
            device_id={"feed": there},
            device_id_type=pl.DeviceIdType.MESH,
        )

    def channelize(k):
        words, out = words_bufs[k], send_bufs[k]
        count = counts[k]

        def block(i, carry):
            base = i * SPAN
            for m in range(SPAN + TAPS - 1):
                voltage[m * 2 * CH : (m + 1) * 2 * CH, :] = unpack(words[base + m])
            for s in range(SPAN):
                window = voltage[s * 2 * CH : (s + TAPS) * 2 * CH, :]
                parts = jnp.dot(bank, window, preferred_element_type=jnp.float32)
                whole = parts[: 2 * CH]
                for term in range(1, TERMS):
                    whole = whole + parts[2 * CH * term : 2 * CH * (term + 1)]
                real, imag = whole[:CH], whole[CH:]
                upper = gain[0] * real - gain[1] * imag
                lower = gain[0] * imag + gain[1] * real
                for lane in range(rows.shape[1]):
                    place = slice(lane * LANES, (lane + 1) * LANES)
                    rows[0, lane, s * CH : (s + 1) * CH, :] = upper[:, place]
                    rows[1, lane, s * CH : (s + 1) * CH, :] = lower[:, place]
            for c in range(CH):
                for part in range(2):
                    where = pl.ds(pl.multiple_of(part * count + base, SPAN), SPAN)
                    for lane in range(rows.shape[1]):
                        width = min(LANES, inputs - lane * LANES)
                        piece = rows[part, lane, pl.ds(c, SPAN, stride=CH), :]
                        out[c, where, lane * LANES : lane * LANES + width] = piece[:, :width].astype(
                            jnp.bfloat16
                        )
            return carry

        lax.fori_loop(0, count // SPAN, block, 0)

    def send(k):
        def one(d, carry):
            remote(k, d).start()
            return carry

        lax.fori_loop(1, size, one, 0)
        own_copy(k).start()

    def arrive(k):
        def one(d, carry):
            remote(k, d).wait_recv()
            return carry

        own_copy(k).wait()
        lax.fori_loop(1, size, one, 0)

    def drain(k):
        def one(d, carry):
            remote(k, d).wait_send()
            return carry

        lax.fori_loop(1, size, one, 0)

    for k in range(chunks):
        word_copy(k).start()
    for k in range(chunks):
        word_copy(k).wait()
        channelize(k)
        if k == 0:
            pl.semaphore_wait(barrier, size - 1)
        send(k)

    feeds = slot_ref.shape[1]
    tile = min(TILE, feeds)
    for k in range(chunks - 1):
        arrive(k)
        depth = 2 * counts[k]
        set_left(left, hold_bufs[k], own_ref[...], scale)

        def columns(j, carry, k=k, depth=depth):
            where = pl.ds(pl.multiple_of(j * tile, tile), tile)
            ordered = pick(hold_bufs[k], slot_ref[:, where]).astype(jnp.bfloat16)
            for part in range(2):
                product = jnp.dot(left[part, :, :depth], ordered, preferred_element_type=jnp.float32)
                if k:
                    product = product + total[part, :, where]
                total[part, :, where] = product
            return carry

        lax.fori_loop(0, feeds // tile, columns, 0)
    total_copy = pltpu.make_async_copy(total, total_hbm, total_sem)
    total_copy.start()
    arrive(chunks - 1)
    for k in range(chunks):
        drain(k)
    total_copy.wait()


def exchange(words, gains, feed_slot, own, counts, inputs, groups, scale):
    size = CH * groups
    feeds = feed_slot.shape[0]
    wide = words.shape[2]
    bank = jnp.asarray(filter_bank())
    held = [jax.ShapeDtypeStruct((size, 2 * count, inputs), jnp.bfloat16) for count in counts]
    memory = pl.BlockSpec(memory_space=pltpu.VMEM)
    anywhere = pl.BlockSpec(memory_space=pl.ANY)
    chunks = len(counts)
    return pl.pallas_call(
        functools.partial(exchange_kernel, counts, groups, scale),
        out_shape=(held[-1], jax.ShapeDtypeStruct((2, ROWS, feeds), jnp.float32)),
        in_specs=[memory, anywhere, memory, memory, memory],
        out_specs=(anywhere, anywhere),
        scratch_shapes=[pltpu.VMEM((count + TAPS - 1, CH, wide), jnp.int32) for count in counts]
        + [pltpu.VMEM((CH, 2 * count, inputs), jnp.bfloat16) for count in counts]
        + [pltpu.VMEM(one.shape, one.dtype) for one in held[:-1]]
        + [
            pltpu.VMEM(((SPAN + TAPS) * 2 * CH, wide), jnp.bfloat16),
            pltpu.VMEM((2, wide // LANES, SPAN * CH, LANES), jnp.float32),
            pltpu.VMEM((2, ROWS, feeds), jnp.float32),
            pltpu.VMEM((2, ROWS, 2 * max(counts)), jnp.bfloat16),
            pltpu.SemaphoreType.DMA((chunks,)),
            pltpu.SemaphoreType.DMA((chunks,)),
            pltpu.SemaphoreType.DMA,
            pltpu.SemaphoreType.DMA((chunks, size)),
            pltpu.SemaphoreType.DMA((chunks, size)),
        ],
        compiler_params=pltpu.CompilerParams(
            collective_id=0, has_side_effects=True, vmem_limit_bytes=60 * 2**20
        ),
    )(bank, words, gains, feed_slot[None], own[None])


def finish_kernel(scale, moved_ref, slot_ref, own_ref, total_ref, out_ref, left):
    @pl.when(pl.program_id(0) == 0)
    def _():
        set_left(left, moved_ref, own_ref[...], scale)

    ordered = pick(moved_ref, slot_ref[...]).astype(jnp.bfloat16)
    for part in range(2):
        product = jnp.dot(left[part], ordered, preferred_element_type=jnp.float32)
        out_ref[:, part, :] = product + total_ref[part]


def finish(moved, feed_slot, own, total, scale):
    feeds = feed_slot.shape[0]
    tile = min(TILE, feeds)
    return pl.pallas_call(
        functools.partial(finish_kernel, scale),
        out_shape=jax.ShapeDtypeStruct((ROWS, 2, feeds), jnp.float32),
        grid=(feeds // tile,),
        in_specs=[
            pl.BlockSpec(moved.shape, lambda j: (0, 0, 0)),
            pl.BlockSpec((1, tile), lambda j: (0, j)),
            pl.BlockSpec((1, ROWS), lambda j: (0, 0)),
            pl.BlockSpec((2, ROWS, tile), lambda j: (0, 0, j)),
        ],
        out_specs=pl.BlockSpec((ROWS, 2, tile), lambda j: (0, 0, j)),
        scratch_shapes=[pltpu.VMEM((2, ROWS, moved.shape[1]), jnp.bfloat16)],
    )(moved, feed_slot[None], own[None], total)


def body(samples, gains, feed_slot):
    groups = lax.axis_size("feed") // CH
    first = lax.axis_index("feed") % groups * ROWS
    inputs = samples.shape[0]
    spectra = samples.shape[2] - TAPS + 1
    counts = tuple(spectra * share // sum(SHARES) for share in SHARES)
    words = jnp.transpose(samples, (2, 1, 0))
    spare = -inputs % LANES
    if spare:
        words = jnp.pad(words, ((0, 0), (0, 0), (0, spare)))
        gains = jnp.pad(gains, ((0, 0), (0, 0), (0, spare)))
    own = lax.dynamic_slice_in_dim(feed_slot, first, ROWS, 0)
    scale = 1.0 / spectra
    moved, total = exchange(words, gains, feed_slot, own, counts, inputs, groups, scale)
    return finish(moved, feed_slot, own, total, scale)


def solution(mesh):
    return jax.shard_map(
        body,
        mesh=mesh,
        in_specs=(P(("band", "feed"), None, None), P(None, "band", "feed"), P()),
        out_specs=P(("band", "feed"), None, None),
        check_vma=False,
    )
```

time: 283 us -> 215 us (0.76)
  Pallas kernels: 32 us -> 214 us
  waiting for transfers between devices: 182 us -> 0 us
  local copies, waits for them, and re-layouts: 54.1 us -> 1.27 us
  matrix products: 6.97 us -> 0 us
  starting transfers between devices: 6.65 us -> 0 us
    all_to_all x1 -> x0, waiting for transfers between devices: 182 us -> none  [body(): lax.all_to_all(weighted, 'feed', split_axis=0, concat_axis=0, tiled=True)]
    pallas_call x1 -> x2, Pallas kernels: 32 us -> 214 us  [the longest x1 200 us: exchange(): pl.pallas_call(functools.partial(exchange_kernel, counts, groups, scale),...]
    gather x2 -> x0, local copies, waits for them, and re-layouts: 31.3 us -> none  [the longest x1 25.2 us: body(): ordered = jnp.take(flat, feed_slot, axis=0, mode='clip')]
    unnamed x6 -> x0, local copies, waits for them, and re-layouts: 13 us -> none
    dot_general x1 -> x0, local copies, waits for them, and re-layouts: 9.82 us -> none  [body(): jnp.einsum('rok,jk->roj', left, ordered, preferred_element_type=jnp.float32)]
    dot_general x1 -> x0, matrix products: 6.97 us -> none  [body(): jnp.einsum('rok,jk->roj', left, ordered, preferred_element_type=jnp.float32)]
    all_to_all x1 -> x0, starting transfers between devices: 6.65 us -> none  [body(): lax.all_to_all(weighted, 'feed', split_axis=0, concat_axis=0, tiled=True)]
  transfers between devices with their start and end apart: 1 -> 0, of which waited for: 1 -> 0; matrix products, arithmetic and copies ran while one was open for 0% -> 0% of each run, Pallas kernels for 0% -> 0%
where the time goes in v3:
time: 215 us
  Pallas kernels  214 us (100%)
    pallas_call x1, Pallas kernels, exchange(): pl.pallas_call(functools.partial(exchange_kernel, counts, groups, scale),...  200 us
    pallas_call x1, Pallas kernels, finish(): pl.pallas_call(functools.partial(finish_kernel, scale), out_shape=jax.Sha...  13.8 us

profile of v3, /device:TPU:13, one launch (start us, length us, event | category | flops | bytes accessed | tf_op | source)
XLA Modules:
  0.0 215.0 jit_solution(1317333146116813871)
XLA Ops:
  0.0 1.3 dynamic_slice.3
  1.3 199.9 %shard_map.46 = (bf16[16,128,256]{2,1,0:T(8,128)(2,1)}, f32[2,256,4096]{2,1,0:T(8,128)}) custom-call(bf16[96,256]{1,0:T(8,128)(2,1)} %constant.20.clone.bank_ref, s32[519,16,256]{2,1,0:T(8,128)} %bitcast.3, s32[2,16,256]{2,1,0:T(8,128)} %gains_ref.1, s32[1,4096]{1,0:T(1,128)} %bitcast.4, s32[1,256]{1,0:T(1,128)} %bitcast.6), custom_call_target="tpu_custom_call" | custom-call | tf_op jit(solution)/shard_map/pallas_call | solution.py:211
  201.2 13.8 %shard_map.47 = f32[256,2,4096]{2,1,0:T(2,128)} custom-call(bf16[16,128,256]{2,1,0:T(8,128)(2,1)} %get-tuple-element.7.moved_ref, s32[1,4096]{1,0:T(1,128)} %bitcast.5, s32[1,256]{1,0:T(1,128)} %bitcast.7, f32[2,256,4096]{2,1,0:T(8,128)} %get-tuple-element.8.total_ref), custom_call_target="tpu_custom_call" | custom-call | tf_op jit(solution)/shard_map/pallas_call | solution.py:250

commit v4 on v3

--- a/solution.py
+++ b/solution.py
@@ -57,22 +57,22 @@
     return total
 
 
-def set_left(left, moved_ref, columns, scale):
-    depth = moved_ref.shape[1]
-    feed_rows = jnp.transpose(pick(moved_ref, columns)) * scale
+def set_left(left, feed_columns, scale):
+    depth = feed_columns.shape[0]
+    feed_rows = jnp.transpose(feed_columns) * scale
     real, imag = feed_rows[:, : depth // 2], feed_rows[:, depth // 2 :]
     left[0, :, :depth] = jnp.concatenate([real, imag], axis=1).astype(jnp.bfloat16)
     left[1, :, :depth] = jnp.concatenate([imag, -real], axis=1).astype(jnp.bfloat16)
 
 
-def exchange_kernel(counts, groups, scale, bank_ref, words_hbm, gains_ref, slot_ref, own_ref, *refs):
+def exchange_kernel(counts, groups, scale, bank_ref, words_hbm, gains_ref, slot_ref, *refs):
     chunks = len(counts)
-    last_hbm, total_hbm = refs[:2]
+    ordered_ref, total_hbm = refs[:2]
     words_bufs = refs[2 : 2 + chunks]
     send_bufs = refs[2 + chunks : 2 + 2 * chunks]
-    hold_bufs = refs[2 + 2 * chunks : 1 + 3 * chunks]
-    voltage, rows, total, left, word_sem, own_sem, total_sem, send_sem, recv_sem = refs[1 + 3 * chunks :]
-    targets = hold_bufs + (last_hbm,)
+    hold_bufs = refs[2 + 2 * chunks : 2 + 3 * chunks]
+    voltage, rows, total, left, gathered = refs[2 + 3 * chunks : 7 + 3 * chunks]
+    word_sem, own_sem, total_sem, send_sem, recv_sem = refs[7 + 3 * chunks :]
     me = lax.axis_index("feed")
     size = lax.axis_size("feed")
     inputs = send_bufs[0].shape[2]
@@ -94,13 +94,13 @@
         return pltpu.make_async_copy(source, words_bufs[k], word_sem.at[k])
 
     def own_copy(k):
-        return pltpu.make_async_copy(send_bufs[k].at[me // groups], targets[k].at[me], own_sem.at[k])
+        return pltpu.make_async_copy(send_bufs[k].at[me // groups], hold_bufs[k].at[me], own_sem.at[k])
 
     def remote(k, d):
         there = (me + d) % size
         return pltpu.make_async_remote_copy(
             src_ref=send_bufs[k].at[there // groups],
-            dst_ref=targets[k].at[me],
+            dst_ref=hold_bufs[k].at[me],
             send_sem=send_sem.at[k, d],
             recv_sem=recv_sem.at[k, d],
             device_id={"feed": there},
@@ -175,10 +175,11 @@
 
     feeds = slot_ref.shape[1]
     tile = min(TILE, feeds)
+    own = pl.ds(pl.multiple_of(me % groups * ROWS, ROWS), ROWS)
     for k in range(chunks - 1):
         arrive(k)
         depth = 2 * counts[k]
-        set_left(left, hold_bufs[k], own_ref[...], scale)
+        set_left(left, pick(hold_bufs[k], slot_ref[:, own]), scale)
 
         def columns(j, carry, k=k, depth=depth):
             where = pl.ds(pl.multiple_of(j * tile, tile), tile)
@@ -193,13 +194,38 @@
         lax.fori_loop(0, feeds // tile, columns, 0)
     total_copy = pltpu.make_async_copy(total, total_hbm, total_sem)
     total_copy.start()
-    arrive(chunks - 1)
+    last = chunks - 1
+
+    def scatter(d, fresh):
+        source = (me - d + size) % size
+        arrived = hold_bufs[last][source]
+
+        def columns(j, carry):
+            where = pl.ds(pl.multiple_of(j * tile, tile), tile)
+            place = lax.broadcasted_iota(jnp.int32, (inputs, tile), 0) + source * inputs
+            hot = jnp.where(place == slot_ref[:, where], 1.0, 0.0).astype(jnp.bfloat16)
+            part = jnp.dot(arrived, hot, preferred_element_type=jnp.float32)
+            gathered[:, where] = part if fresh else gathered[:, where] + part
+            return carry
+
+        lax.fori_loop(0, feeds // tile, columns, 0)
+
+    own_copy(last).wait()
+    scatter(0, True)
+
+    def follow(d, carry):
+        remote(last, d).wait_recv()
+        scatter(d, False)
+        return carry
+
+    lax.fori_loop(1, size, follow, 0)
+    ordered_ref[...] = gathered[...].astype(jnp.bfloat16)
     for k in range(chunks):
         drain(k)
     total_copy.wait()
 
 
-def exchange(words, gains, feed_slot, own, counts, inputs, groups, scale):
+def exchange(words, gains, feed_slot, counts, inputs, groups, scale):
     size = CH * groups
     feeds = feed_slot.shape[0]
     wide = words.shape[2]
@@ -210,17 +236,18 @@
     chunks = len(counts)
     return pl.pallas_call(
         functools.partial(exchange_kernel, counts, groups, scale),
-        out_shape=(held[-1], jax.ShapeDtypeStruct((2, ROWS, feeds), jnp.float32)),
-        in_specs=[memory, anywhere, memory, memory, memory],
-        out_specs=(anywhere, anywhere),
+        out_shape=(jax.ShapeDtypeStruct((2 * counts[-1], feeds), jnp.bfloat16), jax.ShapeDtypeStruct((2, ROWS, feeds), jnp.float32)),
+        in_specs=[memory, anywhere, memory, memory],
+        out_specs=(memory, anywhere),
         scratch_shapes=[pltpu.VMEM((count + TAPS - 1, CH, wide), jnp.int32) for count in counts]
         + [pltpu.VMEM((CH, 2 * count, inputs), jnp.bfloat16) for count in counts]
-        + [pltpu.VMEM(one.shape, one.dtype) for one in held[:-1]]
+        + [pltpu.VMEM(one.shape, one.dtype) for one in held]
         + [
             pltpu.VMEM(((SPAN + TAPS) * 2 * CH, wide), jnp.bfloat16),
             pltpu.VMEM((2, wide // LANES, SPAN * CH, LANES), jnp.float32),
             pltpu.VMEM((2, ROWS, feeds), jnp.float32),
             pltpu.VMEM((2, ROWS, 2 * max(counts)), jnp.bfloat16),
+            pltpu.VMEM((2 * counts[-1], feeds), jnp.float32),
             pltpu.SemaphoreType.DMA((chunks,)),
             pltpu.SemaphoreType.DMA((chunks,)),
             pltpu.SemaphoreType.DMA,
@@ -230,41 +257,40 @@
         compiler_params=pltpu.CompilerParams(
             collective_id=0, has_side_effects=True, vmem_limit_bytes=60 * 2**20
         ),
-    )(bank, words, gains, feed_slot[None], own[None])
-
-
-def finish_kernel(scale, moved_ref, slot_ref, own_ref, total_ref, out_ref, left):
+    )(bank, words, gains, feed_slot[None])
+
+
+def finish_kernel(groups, scale, whole_ref, ordered_ref, total_ref, out_ref, left):
     @pl.when(pl.program_id(0) == 0)
     def _():
-        set_left(left, moved_ref, own_ref[...], scale)
-
-    ordered = pick(moved_ref, slot_ref[...]).astype(jnp.bfloat16)
+        first = 0 if groups == 1 else lax.axis_index("feed") % groups * ROWS
+        own = pl.ds(pl.multiple_of(first, ROWS), ROWS)
+        set_left(left, whole_ref[:, own].astype(jnp.float32), scale)
+
     for part in range(2):
-        product = jnp.dot(left[part], ordered, preferred_element_type=jnp.float32)
+        product = jnp.dot(left[part], ordered_ref[...], preferred_element_type=jnp.float32)
         out_ref[:, part, :] = product + total_ref[part]
 
 
-def finish(moved, feed_slot, own, total, scale):
-    feeds = feed_slot.shape[0]
+def finish(ordered, total, groups, scale):
+    depth, feeds = ordered.shape
     tile = min(TILE, feeds)
     return pl.pallas_call(
-        functools.partial(finish_kernel, scale),
+        functools.partial(finish_kernel, groups, scale),
         out_shape=jax.ShapeDtypeStruct((ROWS, 2, feeds), jnp.float32),
         grid=(feeds // tile,),
         in_specs=[
-            pl.BlockSpec(moved.shape, lambda j: (0, 0, 0)),
-            pl.BlockSpec((1, tile), lambda j: (0, j)),
-            pl.BlockSpec((1, ROWS), lambda j: (0, 0)),
+            pl.BlockSpec((depth, feeds), lambda j: (0, 0)),
+            pl.BlockSpec((depth, tile), lambda j: (0, j)),
             pl.BlockSpec((2, ROWS, tile), lambda j: (0, 0, j)),
         ],
         out_specs=pl.BlockSpec((ROWS, 2, tile), lambda j: (0, 0, j)),
-        scratch_shapes=[pltpu.VMEM((2, ROWS, moved.shape[1]), jnp.bfloat16)],
-    )(moved, feed_slot[None], own[None], total)
+        scratch_shapes=[pltpu.VMEM((2, ROWS, depth), jnp.bfloat16)],
+    )(ordered, ordered, total)
 
 
 def body(samples, gains, feed_slot):
     groups = lax.axis_size("feed") // CH
-    first = lax.axis_index("feed") % groups * ROWS
     inputs = samples.shape[0]
     spectra = samples.shape[2] - TAPS + 1
     counts = tuple(spectra * share // sum(SHARES) for share in SHARES)
@@ -273,10 +299,9 @@
     if spare:
         words = jnp.pad(words, ((0, 0), (0, 0), (0, spare)))
         gains = jnp.pad(gains, ((0, 0), (0, 0), (0, spare)))
-    own = lax.dynamic_slice_in_dim(feed_slot, first, ROWS, 0)
     scale = 1.0 / spectra
-    moved, total = exchange(words, gains, feed_slot, own, counts, inputs, groups, scale)
-    return finish(moved, feed_slot, own, total, scale)
+    ordered, total = exchange(words, gains, feed_slot, counts, inputs, groups, scale)
+    return finish(ordered, total, groups, scale)
 
 
 def solution(mesh):

time: 215 us -> 235 us (1.093)
  Pallas kernels: 214 us -> 234 us
    pallas_call x1, Pallas kernels: 200 us -> 223 us  [exchange(): pl.pallas_call(functools.partial(exchange_kernel, counts, groups, scale),...]
    pallas_call x1, Pallas kernels: 13.8 us -> 11 us  [finish(): pl.pallas_call(functools.partial(finish_kernel, groups, scale), out_shape...]
where the time goes in v4:
time: 235 us; the launch traced here: 234 us
  Pallas kernels  234 us (100%)
    pallas_call x1, Pallas kernels, exchange(): pl.pallas_call(functools.partial(exchange_kernel, counts, groups, scale),...  223 us
    pallas_call x1, Pallas kernels, finish(): pl.pallas_call(functools.partial(finish_kernel, groups, scale), out_shape...  11 us

profile of v4, /device:TPU:13, one launch (start us, length us, event | category | flops | bytes accessed | tf_op | source)
XLA Modules:
  0.0 234.3 jit_solution(14020285056111059531)
XLA Ops:
  0.0 223.3 %shard_map.46 = (bf16[128,4096]{1,0:T(8,128)(2,1)}, f32[2,256,4096]{2,1,0:T(8,128)}) custom-call(bf16[96,256]{1,0:T(8,128)(2,1)} %constant.2.clone.bank_ref, s32[519,16,256]{2,1,0:T(8,128)} %bitcast.2, s32[2,16,256]{2,1,0:T(8,128)} %gains_ref.1, s32[1,4096]{1,0:T(1,128)} %bitcast.3), custom_call_target="tpu_custom_call" | custom-call | tf_op jit(solution)/shard_map/pallas_call | solution.py:237
  223.3 11.0 %shard_map.47 = f32[256,2,4096]{2,1,0:T(2,128)} custom-call(bf16[128,4096]{1,0:T(8,128)(2,1)} %get-tuple-element.7.whole_ref.ordered_ref, bf16[128,4096]{1,0:T(8,128)(2,1)} %get-tuple-element.7.whole_ref.ordered_ref, f32[2,256,4096]{2,1,0:T(8,128)} %get-tuple-element.8.total_ref), custom_call_target="tpu_custom_call" | custom-call | tf_op jit(solution)/shard_map/pallas_call | solution.py:278
